TPU v7x, 32 devices: a whole 2x2x4 slice. The times are simulated.
32 devices in a mesh: grid: 16 (over z, y, x), band: 2 (over core).
Axes of the slice: x: 2, y: 2, z: 4, core: 2. Of those that a mesh axis runs over, the one named last changes fastest.
Arguments:
- orbitals: float32 [16, 16, 32, 32, 128], P('grid', 'band'), may hold values from -24 to 24, as said below
- potential: float32 [16, 32, 32, 128], P('grid'), may hold values from -1 to 1
Outputs:
- rotated: float32 [16, 16, 32, 32, 128], P('grid', 'band')
Inputs may be any that keep to these rules, and one draw needn't show every extreme that they name: `orbitals`: real-valued orbital samples.
All inputs are finite; a program needn't handle non-finite values.
Results may differ from a plain program's by a relative error of at most 0.00013.
Values sent between devices are 32-bit elements; how exact they have to be, the bound alone decides.
A program may use at most 128 MiB of HBM per device.

v0:
```python
import jax
import jax.numpy as jnp
from jax import lax
from jax.sharding import PartitionSpec as P

COEFFS = (-49.0 / 18.0, 1.5, -0.15, 1.0 / 90.0)
CENTER = 5.75
HALF_WIDTH = 4.75


def shifted(value, axis, steps):
    count = lax.axis_size(axis)
    leading, last = (max(0, -steps), min(count, count - steps))
    return lax.ppermute(value, axis, [(source, source + steps) for source in range(leading, last)])


def layout():
    devices_grid = lax.axis_size("grid")
    parts_x = max(2, devices_grid // 32)
    parts_z = devices_grid // (parts_x * parts_x)
    return (parts_x, parts_x, parts_z)


def neighbour(face_block, stride, keep_it):
    moved = shifted(face_block.reshape(face_block.shape[0], -1), "grid", stride)
    return jnp.where(keep_it, moved, 0.0).reshape(face_block.shape)


def apply_hamil(values_in, local_potential):
    parts_x, parts_y, parts_z = layout()
    grid_index = lax.axis_index("grid")
    pos_z = grid_index % parts_z
    pos_y = grid_index // parts_z % parts_y
    reach_max = len(COEFFS) - 1
    padded = jnp.pad(
        values_in, ((0, 0), (reach_max, reach_max), (reach_max, reach_max), (reach_max, reach_max))
    )
    plan = (
        (1, parts_y * parts_z, True, True),
        (2, parts_z, pos_y > 0, pos_y < parts_y - 1),
        (3, 1, pos_z > 0, pos_z < parts_z - 1),
    )
    for dim_index, stride, keep_lower, keep_upper in plan:
        extent = values_in.shape[dim_index]
        lower_face = neighbour(
            lax.slice_in_dim(values_in, extent - reach_max, extent, axis=dim_index),
            stride,
            keep_lower,
        )
        upper_face = neighbour(
            lax.slice_in_dim(values_in, 0, reach_max, axis=dim_index), -stride, keep_upper
        )
        lower_start = [0, reach_max, reach_max, reach_max]
        upper_start = [0, reach_max, reach_max, reach_max]
        lower_start[dim_index] = 0
        upper_start[dim_index] = reach_max + extent
        padded = lax.dynamic_update_slice(padded, lower_face, lower_start)
        padded = lax.dynamic_update_slice(padded, upper_face, upper_start)
    summed = 3.0 * COEFFS[0] * values_in
    for dim_index in range(1, 4):
        extent = values_in.shape[dim_index]
        for reach in range(1, reach_max + 1):
            upper_start = [0, reach_max, reach_max, reach_max]
            lower_start = [0, reach_max, reach_max, reach_max]
            upper_start[dim_index] = reach_max + reach
            lower_start[dim_index] = reach_max - reach
            upper_part = lax.slice(
                padded, upper_start, [upper_start[k] + values_in.shape[k] for k in range(4)]
            )
            lower_part = lax.slice(
                padded, lower_start, [lower_start[k] + values_in.shape[k] for k in range(4)]
            )
            summed = summed + COEFFS[reach] * (upper_part + lower_part)
    return -0.5 * summed + local_potential[None] * values_in


def chebyshev(start_block, local_potential):
    first_term = (apply_hamil(start_block, local_potential) - CENTER * start_block) / HALF_WIDTH
    return (
        2.0 * (apply_hamil(first_term, local_potential) - CENTER * first_term) / HALF_WIDTH
        - start_block
    )


def on_device(orbitals, potential):
    local_block = orbitals[0]
    local_potential = potential[0]
    band_index = lax.axis_index("band")
    local_count = local_block.shape[0]
    own_filtered = chebyshev(local_block, local_potential)
    gathered = lax.all_gather(own_filtered, "band", axis=0, tiled=True)
    total_orbs = gathered.shape[0]
    flat_all = gathered.reshape(total_orbs, -1)
    volume = flat_all.shape[1] * lax.axis_size("grid")
    partial_value = jnp.einsum("ic,jc->ij", flat_all, flat_all, precision=lax.Precision.HIGHEST)
    gram = lax.psum(partial_value, "grid")
    gram = gram / volume
    factor = jnp.linalg.cholesky(gram)
    weights = jax.scipy.linalg.solve_triangular(
        factor, jnp.eye(total_orbs, dtype=jnp.float32), lower=True
    )
    weight_rows = lax.dynamic_slice_in_dim(weights, band_index * local_count, local_count, 0)
    rotated = jnp.dot(
        weight_rows, flat_all, precision=lax.Precision.HIGHEST, preferred_element_type=jnp.float32
    )
    return rotated.reshape(local_block.shape)[None]


def solution(mesh):
    in_specs = (P("grid", "band", None, None, None), P("grid", None, None, None))
    out_specs = P("grid", "band", None, None, None)
    return jax.shard_map(
        on_device, mesh=mesh, in_specs=in_specs, out_specs=out_specs, check_vma=False
    )
```

profile of v0, /device:TPU:0, one launch (start us, length us, event | category | flops | bytes accessed | tf_op | source)
XLA Modules:
  0.0 975.7 jit_solution(6393854721621182004)
XLA Ops:
  6.5 6.0 copy.68
  12.5 1.0 fusion.61
  13.6 5.7 collective-permute-start.2
  20.2 4.5 collective-permute-start
  24.7 1.3 collective-permute-start.1
  26.0 1.3 collective-permute-start.3
  27.3 4.7 fusion.60
  32.0 8.5 copy.22
  40.6 1.7 reshape.98
  42.3 2.5 copy.23
  44.7 4.0 collective-permute-start.4
  48.9 9.1 pad.7
  58.0 8.5 copy.26
  66.5 1.6 reshape.100
  68.2 1.8 copy.27
  70.0 1.6 collective-permute-start.5
  71.6 6.2 reshape.117
  77.8 7.9 copy.25
  85.7 6.2 reshape.118
  91.9 17.1 %copy.29 = f32[8,32,32,3]{3,0,2,1:T(8,128)} copy(f32[8,32,32,3]{3,2,1,0:T(8,128)} %reshape.118) | data formatting | bytes 196608 | tf_op jit(solution)/shard_map/reshape | solution.py:26
  109.1 17.4 %dynamic_update_slice.36 = f32[8,38,38,134]{3,0,2,1:T(8,128)} dynamic-update-slice(f32[8,38,38,134]{3,0,2,1:T(8,128)} %pad.7, f32[8,3,32,128]{3,0,2,1:T(8,128)} %bitcast.2, s32[]{:T(128)} %constant.106.clone.1, s32[]{:T(128)} %constant.106.clone.1, s32[]{:T(128)} %constant.107.clone.1, s32[]{:T(128)} %constant.107.clone.1) | dynamic-update-slice | bytes 786436 | tf_op jit(solution)/shard_map/dynamic_update_slice | solution.py:57
  126.4 17.7 %dynamic_update_slice.37 = f32[8,38,38,134]{3,0,2,1:T(8,128)} dynamic-update-slice(f32[8,38,38,134]{3,0,2,1:T(8,128)} %dynamic_update_slice.36, f32[8,3,32,128]{3,0,2,1:T(8,128)S(1)} %bitcast.78, s32[]{:T(128)} %constant.106.clone.1, s32[]{:T(128)} %constant.108.clone.1, s32[]{:T(128)} %constant.107.clone.1, s32[]{:T(128)} %constant.107.clone.1) | dynamic-update-slice | bytes 786436 | tf_op jit(solution)/shard_map/dynamic_update_slice | solution.py:58
  144.1 17.8 %dynamic_update_slice.38 = f32[8,38,38,134]{3,0,2,1:T(8,128)} dynamic-update-slice(f32[8,38,38,134]{3,0,2,1:T(8,128)} %dynamic_update_slice.37, f32[8,32,3,128]{3,0,2,1:T(8,128)S(1)} %bitcast.75, s32[]{:T(128)} %constant.106.clone.1, s32[]{:T(128)} %constant.107.clone.1, s32[]{:T(128)} %constant.106.clone.1, s32[]{:T(128)} %constant.107.clone.1) | dynamic-update-slice | bytes 786436 | tf_op jit(solution)/shard_map/dynamic_update_slice | solution.py:57
  163.0 17.9 %dynamic_update_slice.39 = f32[8,38,38,134]{3,0,2,1:T(8,128)} dynamic-update-slice(f32[8,38,38,134]{3,0,2,1:T(8,128)} %dynamic_update_slice.38, f32[8,32,3,128]{3,0,2,1:T(8,128)S(1)} %bitcast.77, s32[]{:T(128)} %constant.106.clone.1, s32[]{:T(128)} %constant.107.clone.1, s32[]{:T(128)} %constant.108.clone.1, s32[]{:T(128)} %constant.107.clone.1) | dynamic-update-slice | bytes 786436 | tf_op jit(solution)/shard_map/dynamic_update_slice | solution.py:58
  180.8 28.3 %dynamic_update_slice.40 = f32[8,38,38,134]{3,0,2,1:T(8,128)} dynamic-update-slice(f32[8,38,38,134]{3,0,2,1:T(8,128)} %dynamic_update_slice.39, f32[8,32,32,3]{3,0,2,1:T(8,128)} %copy.25, s32[]{:T(128)} %constant.106.clone.1, s32[]{:T(128)} %constant.107.clone.1, s32[]{:T(128)} %constant.107.clone.1, s32[]{:T(128)} %constant.106.clone.1) | dynamic-update-slice | bytes 196612 | tf_op jit(solution)/shard_map/dynamic_update_slice | solution.py:57
  209.1 163.7 %dynamic_update_slice.41 = f32[8,38,38,134]{3,0,2,1:T(8,128)} dynamic-update-slice(f32[8,38,38,134]{3,0,2,1:T(8,128)} %dynamic_update_slice.40, f32[8,32,32,3]{3,0,2,1:T(8,128)} %copy.29, s32[]{:T(128)} %constant.106.clone.1, s32[]{:T(128)} %constant.107.clone.1, s32[]{:T(128)} %constant.107.clone.1, s32[]{:T(128)} %constant.115.clone.1) | dynamic-update-slice | bytes 196612 | tf_op jit(solution)/shard_map/dynamic_update_slice | solution.py:58
  372.8 61.8 %broadcast_multiply_fusion = (f32[8,32,32,128]{3,0,2,1:T(8,128)}, f32[8,32,32,128]{3,0,2,1:T(8,128)}) fusion(f32[32,32,128]{2,1,0:T(8,128)S(1)} %bitcast.73, f32[8,38,38,134]{3,0,2,1:T(8,128)} %dynamic_update_slice.41, f32[1,8,32,32,128]{4,3,2,1,0:T(8,128)} %param.2), kind=kLoop, calls=%fused_computation.67 | loop fusion | flops 35651584 | bytes 88604672 | tf_op jit(solution)/shard_map/div | solution.py:78
  434.6 2.1 fusion.59
  436.7 7.9 fusion.57
  444.7 8.5 copy.30
  453.2 2.1 reshape.110
  455.3 1.8 copy.31
  457.1 6.1 collective-permute-start.10
  463.2 2.1 fusion.58
  465.3 9.1 pad.8
  474.4 4.9 collective-permute-start.6
  479.3 1.3 collective-permute-start.7
  480.6 5.4 collective-permute-start.8
  486.0 1.3 collective-permute-start.9
  487.3 8.6 copy.34
  495.9 1.6 reshape.112
  497.5 1.8 copy.35
  499.3 1.3 collective-permute-start.11
  500.7 6.2 reshape.119
  506.9 8.0 copy.33
  514.8 6.2 reshape.120
  521.0 8.1 copy.37
  529.2 17.7 %dynamic_update_slice.42 = f32[8,38,38,134]{3,0,2,1:T(8,128)} dynamic-update-slice(f32[8,38,38,134]{3,0,2,1:T(8,128)} %pad.8, f32[8,3,32,128]{3,0,2,1:T(8,128)S(1)} %bitcast.80, s32[]{:T(128)} %constant.106.clone.1, s32[]{:T(128)} %constant.106.clone.1, s32[]{:T(128)} %constant.107.clone.1, s32[]{:T(128)} %constant.107.clone.1) | dynamic-update-slice | bytes 786436 | tf_op jit(solution)/shard_map/dynamic_update_slice | solution.py:57
  546.9 17.7 %dynamic_update_slice.43 = f32[8,38,38,134]{3,0,2,1:T(8,128)} dynamic-update-slice(f32[8,38,38,134]{3,0,2,1:T(8,128)} %dynamic_update_slice.42, f32[8,3,32,128]{3,0,2,1:T(8,128)S(1)} %bitcast.79, s32[]{:T(128)} %constant.106.clone.1, s32[]{:T(128)} %constant.108.clone.1, s32[]{:T(128)} %constant.107.clone.1, s32[]{:T(128)} %constant.107.clone.1) | dynamic-update-slice | bytes 786436 | tf_op jit(solution)/shard_map/dynamic_update_slice | solution.py:58
  564.6 17.8 %dynamic_update_slice.44 = f32[8,38,38,134]{3,0,2,1:T(8,128)} dynamic-update-slice(f32[8,38,38,134]{3,0,2,1:T(8,128)} %dynamic_update_slice.43, f32[8,32,3,128]{3,0,2,1:T(8,128)S(1)} %bitcast.74, s32[]{:T(128)} %constant.106.clone.1, s32[]{:T(128)} %constant.107.clone.1, s32[]{:T(128)} %constant.106.clone.1, s32[]{:T(128)} %constant.107.clone.1) | dynamic-update-slice | bytes 786436 | tf_op jit(solution)/shard_map/dynamic_update_slice | solution.py:57
  583.5 17.9 %dynamic_update_slice.45 = f32[8,38,38,134]{3,0,2,1:T(8,128)} dynamic-update-slice(f32[8,38,38,134]{3,0,2,1:T(8,128)} %dynamic_update_slice.44, f32[8,32,3,128]{3,0,2,1:T(8,128)S(1)} %bitcast.76, s32[]{:T(128)} %constant.106.clone.1, s32[]{:T(128)} %constant.107.clone.1, s32[]{:T(128)} %constant.108.clone.1, s32[]{:T(128)} %constant.107.clone.1) | dynamic-update-slice | bytes 786436 | tf_op jit(solution)/shard_map/dynamic_update_slice | solution.py:58
  601.3 28.3 %dynamic_update_slice.46 = f32[8,38,38,134]{3,0,2,1:T(8,128)} dynamic-update-slice(f32[8,38,38,134]{3,0,2,1:T(8,128)} %dynamic_update_slice.45, f32[8,32,32,3]{3,0,2,1:T(8,128)} %copy.33, s32[]{:T(128)} %constant.106.clone.1, s32[]{:T(128)} %constant.107.clone.1, s32[]{:T(128)} %constant.107.clone.1, s32[]{:T(128)} %constant.106.clone.1) | dynamic-update-slice | bytes 196612 | tf_op jit(solution)/shard_map/dynamic_update_slice | solution.py:57
  629.6 163.7 %dynamic_update_slice.47 = f32[8,38,38,134]{3,0,2,1:T(8,128)} dynamic-update-slice(f32[8,38,38,134]{3,0,2,1:T(8,128)} %dynamic_update_slice.46, f32[8,32,32,3]{3,0,2,1:T(8,128)} %copy.37, s32[]{:T(128)} %constant.106.clone.1, s32[]{:T(128)} %constant.107.clone.1, s32[]{:T(128)} %constant.107.clone.1, s32[]{:T(128)} %constant.115.clone.1) | dynamic-update-slice | bytes 196612 | tf_op jit(solution)/shard_map/dynamic_update_slice | solution.py:58
  793.3 62.5 %fusion.8 = f32[8,32,32,128]{3,0,2,1:T(8,128)} fusion(f32[8,38,38,134]{3,0,2,1:T(8,128)} %dynamic_update_slice.47, f32[8,32,32,128]{3,0,2,1:T(8,128)} %get-tuple-element.6, f32[32,32,128]{2,1,0:T(8,128)S(1)} %broadcast_multiply_fusion.1, f32[1,8,32,32,128]{4,3,2,1,0:T(8,128)} %param.2), kind=kLoop, calls=%fused_computation.10 | loop fusion | flops 36700160 | bytes 88604672 | tf_op jit(solution)/shard_map/sub | solution.py:80
  855.8 24.7 %all-gather.2.cloned.1.call-done = f32[16,32,32,128]{3,0,2,1:T(8,128)} async-done(((f32[8,32,32,128]{3,0,2,1:T(8,128)}), f32[16,32,32,128]{3,0,2,1:T(8,128)}) %all-gather.2.cloned.1.call-update) | async-done | bytes 8388624 | tf_op jit(solution)/shard_map/all_gather | solution.py:91
  880.5 16.6 %convolution_bitcast_fusion = f32[16,16]{0,1:T(8,128)S(1)} fusion(f32[16,32,32,128]{3,0,2,1:T(8,128)} %all-gather.2.cloned.1.call-done), kind=kOutput, calls=%fused_computation.68 | convolution fusion | flops 402653184 | bytes 8389632 | tf_op jit(solution)/shard_map/ic,jc->ij/dot_general | solution.py:95
  897.0 42.7 %psum.7 = f32[16,16]{0,1:T(8,128)S(1)} all-reduce(f32[16,16]{0,1:T(8,128)S(1)} %convolution_bitcast_fusion), channel_id=1, replica_groups=mesh['grid'=16,'band'=2] {'grid'}, use_global_device_ids=true, to_apply=%region_0.1 | all-reduce | flops 256 | bytes 2048 | tf_op jit(solution)/shard_map/psum | solution.py:96
  939.8 1.5 cholesky.17
  942.6 1.2 custom-call.7
  944.1 6.1 copy.40
  950.2 4.9 copy.67
  955.0 1.6 copy.55
  956.6 9.0 fusion.46
  965.7 2.8 copy.42
  (35 shorter events, 4.8 us)
Async XLA Ops:
  6.5 873.9 %all-gather.2.cloned.1.call-start = ((), (), s32[]{:S(2)}) async-start(), calls=%async_computation | async-start | bytes 12582912 | tf_op jit(solution)/shard_map/all_gather | solution.py:91
  12.5 19.5 %copy-start = (f32[1,8,32,32,128]{4,1,3,2,0:T(8,128)}, f32[1,8,32,32,128]{4,1,3,2,0:T(8,128)S(1)}, u32[]{:S(2)}) copy-start(f32[1,8,32,32,128]{4,1,3,2,0:T(8,128)S(1)} %copy.68) | copy-start | bytes 12582916
  13.6 95.4 %collective-permute-start.2 = (f32[8,12288]{1,0:T(8,128)}, f32[8,12288]{1,0:T(8,128)}, u32[]{:S(2)}, u32[]{:S(2)}) collective-permute-start(f32[8,12288]{1,0:T(8,128)} %bitcast.5), channel_id=1, source_target_pairs={{0,8},{2,10},{4,12},{6,14},{8,16},{10,18},{12,20},{14,22},{16,24},... | collective-permute-start | bytes 1179656 | tf_op jit(solution)/shard_map/ppermute | solution.py:14
  20.2 88.9 %collective-permute-start = (f32[8,12288]{1,0:T(8,128)}, f32[8,12288]{1,0:T(8,128)}, u32[]{:S(2)}, u32[]{:S(2)}) collective-permute-start(f32[8,12288]{1,0:T(8,128)} %bitcast.1), channel_id=1, source_target_pairs={{0,16},{2,18},{4,20},{6,22},{8,24},{10,26},{12,28},{14,30},{1,17},... | collective-permute-start | bytes 1179656 | tf_op jit(solution)/shard_map/ppermute | solution.py:14
  24.7 101.7 %collective-permute-start.1 = (f32[8,12288]{1,0:T(8,128)}, f32[8,12288]{1,0:T(8,128)S(1)}, u32[]{:S(2)}, u32[]{:S(2)}) collective-permute-start(f32[8,12288]{1,0:T(8,128)} %bitcast.3), channel_id=1, source_target_pairs={{16,0},{18,2},{20,4},{22,6},{24,8},{26,10},{28,12},{30,14},{17,1},... | collective-permute-start | bytes 1179656 | tf_op jit(solution)/shard_map/ppermute | solution.py:14
  26.0 136.0 %collective-permute-start.3 = (f32[8,12288]{1,0:T(8,128)}, f32[8,12288]{1,0:T(8,128)}, u32[]{:S(2)}, u32[]{:S(2)}) collective-permute-start(f32[8,12288]{1,0:T(8,128)} %bitcast.7), channel_id=1, source_target_pairs={{8,0},{10,2},{12,4},{14,6},{16,8},{18,10},{20,12},{22,14},{24,16},... | collective-permute-start | bytes 1179656 | tf_op jit(solution)/shard_map/ppermute | solution.py:14
  40.6 8.2 copy-start.1
  44.7 25.3 %collective-permute-start.4 = (f32[8,3072]{1,0:T(8,128)}, f32[8,3072]{1,0:T(8,128)}, u32[]{:S(2)}, u32[]{:S(2)}) collective-permute-start(f32[8,3072]{1,0:T(8,128)} %copy.23), channel_id=1, source_target_pairs={{0,2},{2,4},{4,6},{6,8},{8,10},{10,12},{12,14},{14,16},{16,18},{18... | collective-permute-start | bytes 294920 | tf_op jit(solution)/shard_map/ppermute | solution.py:14
  70.0 15.7 %collective-permute-start.5 = (f32[8,3072]{1,0:T(8,128)S(1)}, f32[8,3072]{1,0:T(8,128)S(1)}, u32[]{:S(2)}, u32[]{:S(2)}) collective-permute-start(f32[8,3072]{1,0:T(8,128)S(1)} %copy.27), channel_id=1, source_target_pairs={{2,0},{4,2},{6,4},{8,6},{10,8},{12,10},{14,12},{16,14},{18,16},{20... | collective-permute-start | bytes 294920 | tf_op jit(solution)/shard_map/ppermute | solution.py:14
  457.1 42.2 %collective-permute-start.10 = (f32[8,3072]{1,0:T(8,128)S(1)}, f32[8,3072]{1,0:T(8,128)}, u32[]{:S(2)}, u32[]{:S(2)}) collective-permute-start(f32[8,3072]{1,0:T(8,128)S(1)} %copy.31), channel_id=1, source_target_pairs={{0,2},{2,4},{4,6},{6,8},{8,10},{10,12},{12,14},{14,16},{16,18},{18... | collective-permute-start | bytes 294920 | tf_op jit(solution)/shard_map/ppermute | solution.py:14
  474.4 54.8 %collective-permute-start.6 = (f32[8,12288]{1,0:T(8,128)}, f32[8,12288]{1,0:T(8,128)S(1)}, u32[]{:S(2)}, u32[]{:S(2)}) collective-permute-start(f32[8,12288]{1,0:T(8,128)} %bitcast.10), channel_id=1, source_target_pairs={{0,16},{2,18},{4,20},{6,22},{8,24},{10,26},{12,28},{14,30},{1,17},... | collective-permute-start | bytes 1179656 | tf_op jit(solution)/shard_map/ppermute | solution.py:14
  479.3 67.7 %collective-permute-start.7 = (f32[8,12288]{1,0:T(8,128)}, f32[8,12288]{1,0:T(8,128)S(1)}, u32[]{:S(2)}, u32[]{:S(2)}) collective-permute-start(f32[8,12288]{1,0:T(8,128)} %bitcast.12), channel_id=1, source_target_pairs={{16,0},{18,2},{20,4},{22,6},{24,8},{26,10},{28,12},{30,14},{17,1},... | collective-permute-start | bytes 1179656 | tf_op jit(solution)/shard_map/ppermute | solution.py:14
  480.6 48.6 %collective-permute-start.8 = (f32[8,12288]{1,0:T(8,128)}, f32[8,12288]{1,0:T(8,128)}, u32[]{:S(2)}, u32[]{:S(2)}) collective-permute-start(f32[8,12288]{1,0:T(8,128)} %bitcast.14), channel_id=1, source_target_pairs={{0,8},{2,10},{4,12},{6,14},{8,16},{10,18},{12,20},{14,22},{16,24},... | collective-permute-start | bytes 1179656 | tf_op jit(solution)/shard_map/ppermute | solution.py:14
  486.0 96.4 %collective-permute-start.9 = (f32[8,12288]{1,0:T(8,128)}, f32[8,12288]{1,0:T(8,128)}, u32[]{:S(2)}, u32[]{:S(2)}) collective-permute-start(f32[8,12288]{1,0:T(8,128)} %bitcast.16), channel_id=1, source_target_pairs={{8,0},{10,2},{12,4},{14,6},{16,8},{18,10},{20,12},{22,14},{24,16},... | collective-permute-start | bytes 1179656 | tf_op jit(solution)/shard_map/ppermute | solution.py:14
  499.3 15.5 %collective-permute-start.11 = (f32[8,3072]{1,0:T(8,128)S(1)}, f32[8,3072]{1,0:T(8,128)S(1)}, u32[]{:S(2)}, u32[]{:S(2)}) collective-permute-start(f32[8,3072]{1,0:T(8,128)S(1)} %copy.35), channel_id=1, source_target_pairs={{2,0},{4,2},{6,4},{8,6},{10,8},{12,10},{14,12},{16,14},{18,16},{20... | collective-permute-start | bytes 294920 | tf_op jit(solution)/shard_map/ppermute | solution.py:14
Sparse Core Ops, SparseCore 0:
  855.9 24.4 all-gather.1
where the time goes:
time: 986 us; the launch traced here: 976 us
  local copies, waits for them, and re-layouts  699 us (71%)
  other arithmetic  131 us (13%)
  blocking collectives  42.7 us (4%)
  starting transfers between devices  38.6 us (4%)
  matrix products  25.8 us (3%)
  waiting for transfers between devices  24.7 us (3%)
  between operations  14.2 us (1%)
    dynamic_update_slice x6, local copies, waits for them, and re-layouts, apply_hamil(): padded = lax.dynamic_update_slice(padded, upper_face, upper_start)  398 us
    dynamic_update_slice x6, local copies, waits for them, and re-layouts, apply_hamil(): padded = lax.dynamic_update_slice(padded, lower_face, lower_start)  127 us
    reshape x8, local copies, waits for them, and re-layouts, neighbour(): return jnp.where(keep_it, moved, 0.0).reshape(face_block.shape)  65.9 us
    sub x1, other arithmetic, chebyshev(): 2.0 * (apply_hamil(first_term, local_potential) - CENTER * first_term)  62.5 us
    div x1, other arithmetic, chebyshev(): (apply_hamil(start_block, local_potential) - CENTER * start_block) / HALF...  61.8 us
    psum x1, blocking collectives, on_device(): gram = lax.psum(partial_value, 'grid')  42.7 us
    ppermute x12, starting transfers between devices, shifted(): lax.ppermute(value, axis, [(source, source + steps) for source in range(l...  38.6 us
    slice x8, local copies, waits for them, and re-layouts, apply_hamil(): lax.slice_in_dim(values_in, 0, reach_max, axis=dim_index)  36 us
  transfers between devices with their start and end apart: 13, of which 1 were waited for; matrix products, arithmetic and copies ran while one was open for 24% of the time, Pallas kernels for 0%

commit v1 on v0

--- a/solution.py
+++ b/solution.py
@@ -2,6 +2,7 @@
 import jax.numpy as jnp
 from jax import lax
 from jax.sharding import PartitionSpec as P
+from jax.lax import all_gather
 
 COEFFS = (-49.0 / 18.0, 1.5, -0.15, 1.0 / 90.0)
 CENTER = 5.75
@@ -93,7 +94,12 @@
     flat_all = gathered.reshape(total_orbs, -1)
     volume = flat_all.shape[1] * lax.axis_size("grid")
     partial_value = jnp.einsum("ic,jc->ij", flat_all, flat_all, precision=lax.Precision.HIGHEST)
-    gram = lax.psum(partial_value, "grid")
+
+    def name_the_trails(x0, mesh_name):
+        item_now = all_gather(x0, mesh_name).sum(axis=0)
+        return item_now
+
+    gram = name_the_trails(partial_value, "grid")
     gram = gram / volume
     factor = jnp.linalg.cholesky(gram)
     weights = jax.scipy.linalg.solve_triangular(

time: 986 us -> 985 us (level)
    psum x1 -> x0, blocking collectives: 42.7 us -> none  [on_device(): gram = lax.psum(partial_value, 'grid')]
    all_gather x0 -> x1, blocking collectives: none -> 41.9 us  [name_the_trails(): item_now = all_gather(x0, mesh_name).sum(axis=0)]
where the time goes in v1:
time: 985 us; the launch traced here: 975 us
  local copies, waits for them, and re-layouts  699 us (71%)
  other arithmetic  131 us (13%)
  blocking collectives  41.9 us (4%)
  starting transfers between devices  38.6 us (4%)
  matrix products  25.4 us (3%)
  waiting for transfers between devices  24.7 us (3%)
  between operations  14.1 us (1%)
    dynamic_update_slice x6, local copies, waits for them, and re-layouts, apply_hamil(): padded = lax.dynamic_update_slice(padded, upper_face, upper_start)  398 us
    dynamic_update_slice x6, local copies, waits for them, and re-layouts, apply_hamil(): padded = lax.dynamic_update_slice(padded, lower_face, lower_start)  127 us
    reshape x8, local copies, waits for them, and re-layouts, neighbour(): return jnp.where(keep_it, moved, 0.0).reshape(face_block.shape)  65.9 us
    sub x1, other arithmetic, chebyshev(): 2.0 * (apply_hamil(first_term, local_potential) - CENTER * first_term)  62.5 us
    div x1, other arithmetic, chebyshev(): (apply_hamil(start_block, local_potential) - CENTER * start_block) / HALF...  61.8 us
    all_gather x1, blocking collectives, name_the_trails(): item_now = all_gather(x0, mesh_name).sum(axis=0)  41.9 us
    ppermute x12, starting transfers between devices, shifted(): lax.ppermute(value, axis, [(source, source + steps) for source in range(l...  38.6 us
    slice x8, local copies, waits for them, and re-layouts, apply_hamil(): lax.slice_in_dim(values_in, 0, reach_max, axis=dim_index)  36 us
  transfers between devices with their start and end apart: 13, of which 1 were waited for; matrix products, arithmetic and copies ran while one was open for 24% of the time, Pallas kernels for 0%

profile of v1, /device:TPU:0, one launch (start us, length us, event | category | flops | bytes accessed | tf_op | source)
XLA Modules:
  0.0 974.6 jit_solution(3108298042894450911)
XLA Ops:
  6.5 6.0 copy.64
  12.5 1.0 fusion.61
  13.6 5.7 collective-permute-start.2
  20.2 4.5 collective-permute-start
  24.7 1.3 collective-permute-start.1
  26.0 1.3 collective-permute-start.3
  27.3 4.7 fusion.60
  32.0 8.5 copy.20
  40.6 1.7 reshape.98
  42.3 2.5 copy.21
  44.7 4.0 collective-permute-start.4
  48.9 9.1 pad.7
  58.0 8.5 copy.24
  66.5 1.6 reshape.100
  68.2 1.8 copy.25
  70.0 1.6 collective-permute-start.5
  71.6 6.2 reshape.118
  77.8 7.9 copy.23
  85.7 6.2 reshape.119
  91.9 17.1 %copy.27 = f32[8,32,32,3]{3,0,2,1:T(8,128)} copy(f32[8,32,32,3]{3,2,1,0:T(8,128)} %reshape.119) | data formatting | bytes 196608 | tf_op jit(solution)/shard_map/reshape | solution.py:27
  109.1 17.4 %dynamic_update_slice.36 = f32[8,38,38,134]{3,0,2,1:T(8,128)} dynamic-update-slice(f32[8,38,38,134]{3,0,2,1:T(8,128)} %pad.7, f32[8,3,32,128]{3,0,2,1:T(8,128)} %bitcast.2, s32[]{:T(128)} %constant.107.clone.1, s32[]{:T(128)} %constant.107.clone.1, s32[]{:T(128)} %constant.108.clone.1, s32[]{:T(128)} %constant.108.clone.1) | dynamic-update-slice | bytes 786436 | tf_op jit(solution)/shard_map/dynamic_update_slice | solution.py:58
  126.4 17.7 %dynamic_update_slice.37 = f32[8,38,38,134]{3,0,2,1:T(8,128)} dynamic-update-slice(f32[8,38,38,134]{3,0,2,1:T(8,128)} %dynamic_update_slice.36, f32[8,3,32,128]{3,0,2,1:T(8,128)S(1)} %bitcast.82, s32[]{:T(128)} %constant.107.clone.1, s32[]{:T(128)} %constant.109.clone.1, s32[]{:T(128)} %constant.108.clone.1, s32[]{:T(128)} %constant.108.clone.1) | dynamic-update-slice | bytes 786436 | tf_op jit(solution)/shard_map/dynamic_update_slice | solution.py:59
  144.1 17.8 %dynamic_update_slice.38 = f32[8,38,38,134]{3,0,2,1:T(8,128)} dynamic-update-slice(f32[8,38,38,134]{3,0,2,1:T(8,128)} %dynamic_update_slice.37, f32[8,32,3,128]{3,0,2,1:T(8,128)S(1)} %bitcast.78, s32[]{:T(128)} %constant.107.clone.1, s32[]{:T(128)} %constant.108.clone.1, s32[]{:T(128)} %constant.107.clone.1, s32[]{:T(128)} %constant.108.clone.1) | dynamic-update-slice | bytes 786436 | tf_op jit(solution)/shard_map/dynamic_update_slice | solution.py:58
  163.0 17.9 %dynamic_update_slice.39 = f32[8,38,38,134]{3,0,2,1:T(8,128)} dynamic-update-slice(f32[8,38,38,134]{3,0,2,1:T(8,128)} %dynamic_update_slice.38, f32[8,32,3,128]{3,0,2,1:T(8,128)S(1)} %bitcast.80, s32[]{:T(128)} %constant.107.clone.1, s32[]{:T(128)} %constant.108.clone.1, s32[]{:T(128)} %constant.109.clone.1, s32[]{:T(128)} %constant.108.clone.1) | dynamic-update-slice | bytes 786436 | tf_op jit(solution)/shard_map/dynamic_update_slice | solution.py:59
  180.8 28.3 %dynamic_update_slice.40 = f32[8,38,38,134]{3,0,2,1:T(8,128)} dynamic-update-slice(f32[8,38,38,134]{3,0,2,1:T(8,128)} %dynamic_update_slice.39, f32[8,32,32,3]{3,0,2,1:T(8,128)} %copy.23, s32[]{:T(128)} %constant.107.clone.1, s32[]{:T(128)} %constant.108.clone.1, s32[]{:T(128)} %constant.108.clone.1, s32[]{:T(128)} %constant.107.clone.1) | dynamic-update-slice | bytes 196612 | tf_op jit(solution)/shard_map/dynamic_update_slice | solution.py:58
  209.1 163.7 %dynamic_update_slice.41 = f32[8,38,38,134]{3,0,2,1:T(8,128)} dynamic-update-slice(f32[8,38,38,134]{3,0,2,1:T(8,128)} %dynamic_update_slice.40, f32[8,32,32,3]{3,0,2,1:T(8,128)} %copy.27, s32[]{:T(128)} %constant.107.clone.1, s32[]{:T(128)} %constant.108.clone.1, s32[]{:T(128)} %constant.108.clone.1, s32[]{:T(128)} %constant.116.clone.1) | dynamic-update-slice | bytes 196612 | tf_op jit(solution)/shard_map/dynamic_update_slice | solution.py:59
  372.8 61.8 %broadcast_multiply_fusion = (f32[8,32,32,128]{3,0,2,1:T(8,128)}, f32[8,32,32,128]{3,0,2,1:T(8,128)}) fusion(f32[32,32,128]{2,1,0:T(8,128)S(1)} %bitcast.76, f32[8,38,38,134]{3,0,2,1:T(8,128)} %dynamic_update_slice.41, f32[1,8,32,32,128]{4,3,2,1,0:T(8,128)} %param.2), kind=kLoop, calls=%fused_computation.67 | loop fusion | flops 35651584 | bytes 88604672 | tf_op jit(solution)/shard_map/div | solution.py:79
  434.6 2.1 fusion.59
  436.7 7.9 fusion.57
  444.7 8.5 copy.28
  453.2 2.1 reshape.110
  455.3 1.8 copy.29
  457.1 6.1 collective-permute-start.10
  463.2 2.1 fusion.58
  465.3 9.1 pad.8
  474.4 4.9 collective-permute-start.6
  479.3 1.3 collective-permute-start.7
  480.6 5.4 collective-permute-start.8
  486.0 1.3 collective-permute-start.9
  487.3 8.6 copy.32
  495.9 1.6 reshape.112
  497.5 1.8 copy.33
  499.3 1.3 collective-permute-start.11
  500.7 6.2 reshape.120
  506.9 8.0 copy.31
  514.8 6.2 reshape.121
  521.0 8.1 copy.35
  529.2 17.7 %dynamic_update_slice.42 = f32[8,38,38,134]{3,0,2,1:T(8,128)} dynamic-update-slice(f32[8,38,38,134]{3,0,2,1:T(8,128)} %pad.8, f32[8,3,32,128]{3,0,2,1:T(8,128)S(1)} %bitcast.84, s32[]{:T(128)} %constant.107.clone.1, s32[]{:T(128)} %constant.107.clone.1, s32[]{:T(128)} %constant.108.clone.1, s32[]{:T(128)} %constant.108.clone.1) | dynamic-update-slice | bytes 786436 | tf_op jit(solution)/shard_map/dynamic_update_slice | solution.py:58
  546.9 17.7 %dynamic_update_slice.43 = f32[8,38,38,134]{3,0,2,1:T(8,128)} dynamic-update-slice(f32[8,38,38,134]{3,0,2,1:T(8,128)} %dynamic_update_slice.42, f32[8,3,32,128]{3,0,2,1:T(8,128)S(1)} %bitcast.83, s32[]{:T(128)} %constant.107.clone.1, s32[]{:T(128)} %constant.109.clone.1, s32[]{:T(128)} %constant.108.clone.1, s32[]{:T(128)} %constant.108.clone.1) | dynamic-update-slice | bytes 786436 | tf_op jit(solution)/shard_map/dynamic_update_slice | solution.py:59
  564.6 17.8 %dynamic_update_slice.44 = f32[8,38,38,134]{3,0,2,1:T(8,128)} dynamic-update-slice(f32[8,38,38,134]{3,0,2,1:T(8,128)} %dynamic_update_slice.43, f32[8,32,3,128]{3,0,2,1:T(8,128)S(1)} %bitcast.77, s32[]{:T(128)} %constant.107.clone.1, s32[]{:T(128)} %constant.108.clone.1, s32[]{:T(128)} %constant.107.clone.1, s32[]{:T(128)} %constant.108.clone.1) | dynamic-update-slice | bytes 786436 | tf_op jit(solution)/shard_map/dynamic_update_slice | solution.py:58
  583.5 17.9 %dynamic_update_slice.45 = f32[8,38,38,134]{3,0,2,1:T(8,128)} dynamic-update-slice(f32[8,38,38,134]{3,0,2,1:T(8,128)} %dynamic_update_slice.44, f32[8,32,3,128]{3,0,2,1:T(8,128)S(1)} %bitcast.79, s32[]{:T(128)} %constant.107.clone.1, s32[]{:T(128)} %constant.108.clone.1, s32[]{:T(128)} %constant.109.clone.1, s32[]{:T(128)} %constant.108.clone.1) | dynamic-update-slice | bytes 786436 | tf_op jit(solution)/shard_map/dynamic_update_slice | solution.py:59
  601.3 28.3 %dynamic_update_slice.46 = f32[8,38,38,134]{3,0,2,1:T(8,128)} dynamic-update-slice(f32[8,38,38,134]{3,0,2,1:T(8,128)} %dynamic_update_slice.45, f32[8,32,32,3]{3,0,2,1:T(8,128)} %copy.31, s32[]{:T(128)} %constant.107.clone.1, s32[]{:T(128)} %constant.108.clone.1, s32[]{:T(128)} %constant.108.clone.1, s32[]{:T(128)} %constant.107.clone.1) | dynamic-update-slice | bytes 196612 | tf_op jit(solution)/shard_map/dynamic_update_slice | solution.py:58
  629.6 163.7 %dynamic_update_slice.47 = f32[8,38,38,134]{3,0,2,1:T(8,128)} dynamic-update-slice(f32[8,38,38,134]{3,0,2,1:T(8,128)} %dynamic_update_slice.46, f32[8,32,32,3]{3,0,2,1:T(8,128)} %copy.35, s32[]{:T(128)} %constant.107.clone.1, s32[]{:T(128)} %constant.108.clone.1, s32[]{:T(128)} %constant.108.clone.1, s32[]{:T(128)} %constant.116.clone.1) | dynamic-update-slice | bytes 196612 | tf_op jit(solution)/shard_map/dynamic_update_slice | solution.py:59
  793.3 62.5 %fusion.8 = f32[8,32,32,128]{3,0,2,1:T(8,128)} fusion(f32[8,38,38,134]{3,0,2,1:T(8,128)} %dynamic_update_slice.47, f32[8,32,32,128]{3,0,2,1:T(8,128)} %get-tuple-element.6, f32[32,32,128]{2,1,0:T(8,128)S(1)} %broadcast_multiply_fusion.1, f32[1,8,32,32,128]{4,3,2,1,0:T(8,128)} %param.2), kind=kLoop, calls=%fused_computation.10 | loop fusion | flops 36700160 | bytes 88604672 | tf_op jit(solution)/shard_map/sub | solution.py:81
  855.8 24.7 %all-gather.3.cloned.1.call-done = f32[16,32,32,128]{3,0,2,1:T(8,128)} async-done(((f32[8,32,32,128]{3,0,2,1:T(8,128)}), f32[16,32,32,128]{3,0,2,1:T(8,128)}) %all-gather.3.cloned.1.call-update) | async-done | bytes 8388624 | tf_op jit(solution)/shard_map/all_gather | solution.py:92
  880.5 16.2 %convolution_bitcast_fusion = f32[16,16]{1,0:T(8,128)S(1)} fusion(f32[16,32,32,128]{3,0,2,1:T(8,128)} %all-gather.3.cloned.1.call-done), kind=kOutput, calls=%fused_computation.68 | convolution fusion | flops 402653184 | bytes 8389632 | tf_op jit(solution)/shard_map/ic,jc->ij/dot_general | solution.py:96
  896.6 41.9 %all-gather = f32[256,16]{1,0:T(8,128)S(1)} all-gather(f32[16,16]{1,0:T(8,128)S(1)} %convolution_bitcast_fusion), channel_id=2, replica_groups=mesh['grid'=16,'band'=2] {'grid'}, dimensions={0}, use_global_device_ids=true | all-gather | bytes 17408 | tf_op jit(solution)/shard_map/all_gather | solution.py:99
  938.7 1.5 cholesky.17
  941.5 1.2 custom-call.7
  942.9 6.1 copy.37
  949.0 4.9 copy.63
  953.8 1.6 copy.51
  955.5 9.0 fusion.46
  964.5 2.8 copy.39
  (35 shorter events, 4.8 us)
Async XLA Ops:
  6.5 873.9 %all-gather.3.cloned.1.call-start = ((), (), s32[]{:S(2)}) async-start(), calls=%async_computation | async-start | bytes 12582912 | tf_op jit(solution)/shard_map/all_gather | solution.py:92
  12.5 19.5 %copy-start = (f32[1,8,32,32,128]{4,1,3,2,0:T(8,128)}, f32[1,8,32,32,128]{4,1,3,2,0:T(8,128)S(1)}, u32[]{:S(2)}) copy-start(f32[1,8,32,32,128]{4,1,3,2,0:T(8,128)S(1)} %copy.64) | copy-start | bytes 12582916
  13.6 95.4 %collective-permute-start.2 = (f32[8,12288]{1,0:T(8,128)}, f32[8,12288]{1,0:T(8,128)}, u32[]{:S(2)}, u32[]{:S(2)}) collective-permute-start(f32[8,12288]{1,0:T(8,128)} %bitcast.5), channel_id=1, source_target_pairs={{0,8},{2,10},{4,12},{6,14},{8,16},{10,18},{12,20},{14,22},{16,24},... | collective-permute-start | bytes 1179656 | tf_op jit(solution)/shard_map/ppermute | solution.py:15
  20.2 88.9 %collective-permute-start = (f32[8,12288]{1,0:T(8,128)}, f32[8,12288]{1,0:T(8,128)}, u32[]{:S(2)}, u32[]{:S(2)}) collective-permute-start(f32[8,12288]{1,0:T(8,128)} %bitcast.1), channel_id=1, source_target_pairs={{0,16},{2,18},{4,20},{6,22},{8,24},{10,26},{12,28},{14,30},{1,17},... | collective-permute-start | bytes 1179656 | tf_op jit(solution)/shard_map/ppermute | solution.py:15
  24.7 101.7 %collective-permute-start.1 = (f32[8,12288]{1,0:T(8,128)}, f32[8,12288]{1,0:T(8,128)S(1)}, u32[]{:S(2)}, u32[]{:S(2)}) collective-permute-start(f32[8,12288]{1,0:T(8,128)} %bitcast.3), channel_id=1, source_target_pairs={{16,0},{18,2},{20,4},{22,6},{24,8},{26,10},{28,12},{30,14},{17,1},... | collective-permute-start | bytes 1179656 | tf_op jit(solution)/shard_map/ppermute | solution.py:15
  26.0 136.0 %collective-permute-start.3 = (f32[8,12288]{1,0:T(8,128)}, f32[8,12288]{1,0:T(8,128)}, u32[]{:S(2)}, u32[]{:S(2)}) collective-permute-start(f32[8,12288]{1,0:T(8,128)} %bitcast.7), channel_id=1, source_target_pairs={{8,0},{10,2},{12,4},{14,6},{16,8},{18,10},{20,12},{22,14},{24,16},... | collective-permute-start | bytes 1179656 | tf_op jit(solution)/shard_map/ppermute | solution.py:15
  40.6 8.2 copy-start.1
  44.7 25.3 %collective-permute-start.4 = (f32[8,3072]{1,0:T(8,128)}, f32[8,3072]{1,0:T(8,128)}, u32[]{:S(2)}, u32[]{:S(2)}) collective-permute-start(f32[8,3072]{1,0:T(8,128)} %copy.21), channel_id=1, source_target_pairs={{0,2},{2,4},{4,6},{6,8},{8,10},{10,12},{12,14},{14,16},{16,18},{18... | collective-permute-start | bytes 294920 | tf_op jit(solution)/shard_map/ppermute | solution.py:15
  70.0 15.7 %collective-permute-start.5 = (f32[8,3072]{1,0:T(8,128)S(1)}, f32[8,3072]{1,0:T(8,128)S(1)}, u32[]{:S(2)}, u32[]{:S(2)}) collective-permute-start(f32[8,3072]{1,0:T(8,128)S(1)} %copy.25), channel_id=1, source_target_pairs={{2,0},{4,2},{6,4},{8,6},{10,8},{12,10},{14,12},{16,14},{18,16},{20... | collective-permute-start | bytes 294920 | tf_op jit(solution)/shard_map/ppermute | solution.py:15
  457.1 42.2 %collective-permute-start.10 = (f32[8,3072]{1,0:T(8,128)S(1)}, f32[8,3072]{1,0:T(8,128)}, u32[]{:S(2)}, u32[]{:S(2)}) collective-permute-start(f32[8,3072]{1,0:T(8,128)S(1)} %copy.29), channel_id=1, source_target_pairs={{0,2},{2,4},{4,6},{6,8},{8,10},{10,12},{12,14},{14,16},{16,18},{18... | collective-permute-start | bytes 294920 | tf_op jit(solution)/shard_map/ppermute | solution.py:15
  474.4 54.8 %collective-permute-start.6 = (f32[8,12288]{1,0:T(8,128)}, f32[8,12288]{1,0:T(8,128)S(1)}, u32[]{:S(2)}, u32[]{:S(2)}) collective-permute-start(f32[8,12288]{1,0:T(8,128)} %bitcast.10), channel_id=1, source_target_pairs={{0,16},{2,18},{4,20},{6,22},{8,24},{10,26},{12,28},{14,30},{1,17},... | collective-permute-start | bytes 1179656 | tf_op jit(solution)/shard_map/ppermute | solution.py:15
  479.3 67.7 %collective-permute-start.7 = (f32[8,12288]{1,0:T(8,128)}, f32[8,12288]{1,0:T(8,128)S(1)}, u32[]{:S(2)}, u32[]{:S(2)}) collective-permute-start(f32[8,12288]{1,0:T(8,128)} %bitcast.12), channel_id=1, source_target_pairs={{16,0},{18,2},{20,4},{22,6},{24,8},{26,10},{28,12},{30,14},{17,1},... | collective-permute-start | bytes 1179656 | tf_op jit(solution)/shard_map/ppermute | solution.py:15
  480.6 48.6 %collective-permute-start.8 = (f32[8,12288]{1,0:T(8,128)}, f32[8,12288]{1,0:T(8,128)}, u32[]{:S(2)}, u32[]{:S(2)}) collective-permute-start(f32[8,12288]{1,0:T(8,128)} %bitcast.14), channel_id=1, source_target_pairs={{0,8},{2,10},{4,12},{6,14},{8,16},{10,18},{12,20},{14,22},{16,24},... | collective-permute-start | bytes 1179656 | tf_op jit(solution)/shard_map/ppermute | solution.py:15
  486.0 96.4 %collective-permute-start.9 = (f32[8,12288]{1,0:T(8,128)}, f32[8,12288]{1,0:T(8,128)}, u32[]{:S(2)}, u32[]{:S(2)}) collective-permute-start(f32[8,12288]{1,0:T(8,128)} %bitcast.16), channel_id=1, source_target_pairs={{8,0},{10,2},{12,4},{14,6},{16,8},{18,10},{20,12},{22,14},{24,16},... | collective-permute-start | bytes 1179656 | tf_op jit(solution)/shard_map/ppermute | solution.py:15
  499.3 15.5 %collective-permute-start.11 = (f32[8,3072]{1,0:T(8,128)S(1)}, f32[8,3072]{1,0:T(8,128)S(1)}, u32[]{:S(2)}, u32[]{:S(2)}) collective-permute-start(f32[8,3072]{1,0:T(8,128)S(1)} %copy.33), channel_id=1, source_target_pairs={{2,0},{4,2},{6,4},{8,6},{10,8},{12,10},{14,12},{16,14},{18,16},{20... | collective-permute-start | bytes 294920 | tf_op jit(solution)/shard_map/ppermute | solution.py:15
Sparse Core Ops, SparseCore 0:
  855.9 24.4 all-gather.2
